TPU v7x, 128 devices: a whole 4x4x4 slice. The times are simulated.
128 devices in a mesh: role: 2 (over core), seq: 16 (over z, x), tp: 4 (over y).
Axes of the slice: x: 4, y: 4, z: 4, core: 2. Of those that a mesh axis runs over, the one named last changes fastest.
Arguments:
- merger_hidden: bfloat16 [2048, 5120], P(('role', 'seq'), 'tp'), may hold values from -6 to 6
- merger_out: bfloat16 [5120, 8192], P('tp', ('role', 'seq')), may hold values from -0.078125 to 0.078125
- row_position: int32 [2048], P(('role', 'seq')), may hold values from -1 to 8191, as said below
- prompt_embeds: bfloat16 [8192, 8192], P(('role', 'seq'), 'tp'), may hold values from -300 to 300
- norm_gain: bfloat16 [8192], P('tp'), may hold values from 0.099609375 to 1.8984375
- query_weight: bfloat16 [8192, 4096], P(None, 'tp'), may hold values from -2.762136 to 2.762136
- key_weight: bfloat16 [8192, 512], P(None, 'tp'), may hold values from -0.06629126 to 0.06629126
- value_weight: bfloat16 [8192, 512], P(None, 'tp'), may hold values from -0.0625 to 0.0625
Outputs:
- stream: bfloat16 [8192, 8192], P(('role', 'seq'), 'tp')
- context: bfloat16 [8192, 4096], P(('role', 'seq'), 'tp')
Inputs may be any that keep to these rules, and one draw needn't show every extreme that they name: `row_position`: the live slots of each device's 64 come first and hold distinct prompt positions, distinct over all devices; the other slots hold -1. Of one device's slots at most 4 hold positions of one owner's block (positions j * 256 to (j + 1) * 256 - 1); every device has 4 or more live slots.
All inputs are finite; a program needn't handle non-finite values.
Results may differ from a plain program's by a relative error of at most 0.012.
The roundings to bfloat16 on the way count: a program that leaves them out, or rounds other values in their place, can miss the bound.
Values may be sent and summed in bfloat16 or wider, within the bound.
A program may use at most 192 MiB of HBM per device.

v0:
```python
import math
import jax
import jax.numpy as jnp
from jax import lax
from jax.sharding import PartitionSpec as P

HEAD_DIM = 128


def split_up(x, dim, length):
    before, after = (x.shape[:dim], x.shape[dim + 1 :])
    return jnp.moveaxis(x.reshape(*before, length, -1, *after), dim, 0)


def in_order(blocks, dim):
    lengths = list(blocks.shape[1:])
    lengths[dim] *= blocks.shape[0]
    return jnp.moveaxis(blocks, 0, dim).reshape(lengths)


def exchange_both(x, axis, axes, splits, concats):
    sizes = [lax.axis_size(a) for a in axes]
    blocks = split_up(x, splits[0], sizes[0])
    blocks = jnp.moveaxis(split_up(blocks, splits[1] + 1, sizes[1]), 0, 1)
    inside = blocks.shape[2:]
    blocks = blocks.reshape(-1, *inside)
    blocks = lax.all_to_all(blocks, axis, split_axis=0, concat_axis=0, tiled=True)
    blocks = in_order(blocks.reshape(*sizes, *inside), concats[0] + 1)
    return in_order(blocks, concats[1])


def sent_together(arrays, axis, dim, along):
    widths = [a.shape[along] for a in arrays]
    both = jnp.concatenate(arrays, axis=along)
    filled = lax.all_gather(both, axis, axis=dim, tiled=True)
    return tuple(jnp.split(filled, [sum(widths[:k]) for k in range(1, len(widths))], axis=along))


def rotate(vectors, positions):
    half_dim = vectors.shape[-1] // 2
    frequency = 1000000.0 ** (-jnp.arange(half_dim, dtype=jnp.float32) / half_dim)
    angles = positions.astype(jnp.float32)[:, None, None] * frequency[None, None, :]
    cosine = jnp.cos(angles)
    sine_part = jnp.sin(angles)
    lower_half = vectors[..., :half_dim]
    upper_half = vectors[..., half_dim:]
    return jnp.concatenate(
        [
            lower_half * cosine - upper_half * sine_part,
            upper_half * cosine + lower_half * sine_part,
        ],
        axis=-1,
    )


def sum_hidden(partial_value):
    return lax.psum_scatter(partial_value, "tp", scatter_dimension=1, tiled=True).astype(
        jnp.bfloat16
    )


def project_strips(merger_hidden, merger_out):
    return jnp.dot(
        lax.all_gather(merger_hidden, ("role", "seq"), axis=0, tiled=True),
        merger_out,
        preferred_element_type=jnp.float32,
    )


def body(
    merger_hidden,
    merger_out,
    row_position,
    prompt_embeds,
    norm_gain,
    query_weight,
    key_weight,
    value_weight,
):
    groups = lax.axis_size("role") * lax.axis_size("seq")
    device_rank = lax.axis_index(("role", "seq"))
    row_count = merger_hidden.shape[0]
    tok_count = prompt_embeds.shape[0]
    columns = prompt_embeds.shape[1]
    model_width = columns * lax.axis_size("tp")
    capacity = 2 * row_count // groups
    strips = project_strips(merger_hidden, merger_out)
    partial_value = lax.all_to_all(strips, ("role", "seq"), split_axis=0, concat_axis=1, tiled=True)
    embeds = sum_hidden(partial_value)
    owners = jnp.where(row_position >= 0, row_position // tok_count, groups)
    onehot = (owners[:, None] == jnp.arange(groups, dtype=jnp.int32)[None, :]).astype(jnp.int32)
    earlier = jnp.sum((jnp.cumsum(onehot, axis=0) - onehot) * onehot, axis=1)
    buffer_slot = jnp.where(owners < groups, owners * capacity + earlier, groups * capacity)
    source = (
        jnp.full((groups * capacity,), row_count, jnp.int32)
        .at[buffer_slot]
        .set(jnp.arange(row_count, dtype=jnp.int32), mode="drop")
    )
    padded = jnp.concatenate([embeds, jnp.zeros((1, columns), jnp.bfloat16)], axis=0)
    outgoing = padded[source].reshape(groups, capacity, columns)
    outgoing_pos = jnp.concatenate([row_position, jnp.full((1,), -1, jnp.int32)])[source].reshape(
        groups, capacity
    )
    role_count = lax.axis_size("role")
    seq_count = lax.axis_size("seq")
    arrived, arrived_pos = (
        exchange_both(
            outgoing.reshape(role_count, seq_count, capacity, columns),
            ("role", "seq"),
            ("role", "seq"),
            (0, 1),
            (0, 1),
        ),
        exchange_both(
            outgoing_pos.reshape(role_count, seq_count, capacity),
            ("role", "seq"),
            ("role", "seq"),
            (0, 1),
            (0, 1),
        ),
    )
    arrived_pos = arrived_pos.reshape(-1)
    local_row = jnp.where(arrived_pos >= 0, arrived_pos - device_rank * tok_count, tok_count)
    stream = prompt_embeds.at[local_row].set(arrived.reshape(-1, columns), mode="drop")
    widened = stream.astype(jnp.float32)
    squares = lax.psum(jnp.sum(widened * widened, axis=1), "tp")
    inverse = lax.rsqrt(squares / model_width + 1e-06)[:, None]
    normed = (widened * inverse * norm_gain.astype(jnp.float32)[None, :]).astype(jnp.bfloat16)
    tables = (query_weight, key_weight, value_weight)
    shard_piece = lax.all_gather(normed, "tp", axis=1, tiled=True)
    query_sum, key_sum, value_sum = tuple(
        (jnp.dot(shard_piece, table, preferred_element_type=jnp.float32) for table in tables)
    )
    local_heads = query_weight.shape[1] // HEAD_DIM
    local_kv = key_weight.shape[1] // HEAD_DIM
    group_size = local_heads // local_kv
    positions = device_rank * tok_count + jnp.arange(tok_count, dtype=jnp.int32)
    queries = rotate(query_sum.reshape(tok_count, local_heads, HEAD_DIM), positions).astype(
        jnp.bfloat16
    )
    queries = queries.reshape(tok_count, local_kv, group_size, HEAD_DIM)
    key_rows = rotate(key_sum.reshape(tok_count, local_kv, HEAD_DIM), positions).astype(
        jnp.bfloat16
    )
    value_rows = value_sum.astype(jnp.bfloat16).reshape(tok_count, local_kv, HEAD_DIM)
    score_scale = 1.0 / math.sqrt(HEAD_DIM)
    running_max = jnp.full((local_kv, group_size, tok_count), -1e30, jnp.float32)
    key_piece, value_piece = sent_together((key_rows, value_rows), ("role", "seq"), 0, 1)
    scores = (
        jnp.einsum("qhgd,khd->hgqk", queries, key_piece, preferred_element_type=jnp.float32)
        * score_scale
    )
    key_pos = jnp.arange(key_piece.shape[0], dtype=jnp.int32)
    visible = key_pos[None, :] <= positions[:, None]
    scores = jnp.where(visible, scores, -jnp.inf)
    next_max = jnp.maximum(running_max, jnp.max(scores, axis=3))
    probability = jnp.where(visible, jnp.exp(scores - next_max[..., None]), 0.0)
    running_sum = jnp.sum(probability, axis=3)
    running_out = jnp.einsum(
        "hgqk,khd->hgqd",
        probability.astype(jnp.bfloat16),
        value_piece,
        preferred_element_type=jnp.float32,
    )
    running_max, running_sum, running_out = (next_max, running_sum, running_out)
    context = running_out / running_sum[..., None]
    context = (
        jnp.transpose(context, (2, 0, 1, 3))
        .reshape(tok_count, local_heads * HEAD_DIM)
        .astype(jnp.bfloat16)
    )
    return (stream, context)


def solution(mesh):
    in_specs = (
        P(("role", "seq"), "tp"),
        P("tp", ("role", "seq")),
        P(("role", "seq")),
        P(("role", "seq"), "tp"),
        P("tp"),
        P(None, "tp"),
        P(None, "tp"),
        P(None, "tp"),
    )
    out_specs = (P(("role", "seq"), "tp"), P(("role", "seq"), "tp"))
    return jax.shard_map(body, mesh=mesh, in_specs=in_specs, out_specs=out_specs, check_vma=False)
```

profile of v0, /device:TPU:1, one launch (start us, length us, event | category | flops | bytes accessed | tf_op | source)
XLA Modules:
  0.0 347.9 jit_solution(12780545009831213138)
XLA Ops:
  7.2 0.0 copy-start
  7.2 0.0 all-gather.4.cloned.1.call-start
  7.2 0.7 all-gather.4.cloned.1.call-update
  7.9 0.0 reduce-scatter.2.cloned.1.call-start
  8.0 53.5 %all-gather.4.cloned.1.call-done = bf16[2048,1280]{1,0:T(8,128)(2,1)} async-done(((bf16[64,1280]{1,0:T(8,128)(2,1)}), bf16[2048,1280]{1,0:T(8,128)(2,1)}) %all-gather.4.cloned.1.call-update) | async-done | bytes 5242896 | tf_op jit(solution)/shard_map/all_gather | solution.py:64
  61.5 4.2 %fusion.35 = f32[2048,256]{1,0:T(8,128)S(1)} fusion(bf16[2048,1280]{1,0:T(8,128)(2,1)} %all-gather.4.cloned.1.call-done, bf16[1280,256]{1,0:T(8,128)(2,1)} %param.9), kind=kOutput, calls=%fused_computation.73 | convolution fusion | flops 1342177280 | bytes 7995392 | tf_op jit(solution)/shard_map/dot_general | solution.py:63
  65.7 32.9 %all_to_all.29 = f32[32,64,256]{2,1,0:T(8,128)S(1)} all-to-all(f32[32,64,256]{2,1,0:T(8,128)S(1)} %bitcast.88), channel_id=1, replica_groups=mesh['role'=2,'seq'=16,'tp'=4] {'role','seq'}, dimensions={0} | all-to-all | bytes 4194304 | tf_op jit(solution)/shard_map/all_to_all | solution.py:88
  98.5 0.0 copy-start.6
  98.5 1.5 copy.49
  100.0 0.0 reduce-scatter.2.cloned.1.call-update
  100.1 0.0 copy-done.6
  100.1 0.1 fusion.25
  100.2 0.1 reduce_window_sum.11
  100.3 0.2 select_reduce_fusion
  100.5 0.8 scatter_custom_fusion
  101.3 0.1 pad_add_fusion
  101.4 1.2 gather_fusion
  102.6 0.0 copy-start.5
  102.6 0.7 reshape_transpose_transpose_reshape_reshape_reshape_reshape.6
  103.3 5.1 %all-to-all-start = ((s32[32,1,1,4]{3,2,1,0:T(1,128)}), s32[32,1,1,4]{3,2,1,0:T(1,128)S(1)}, u32[]{:S(2)}, u32[]{:S(2)}) async-start(s32[32,1,1,4]{3,2,1,0:T(1,128)} %bitcast), calls=%async_computation | async-start | bytes 32768 | tf_op jit(solution)/shard_map/all_to_all | solution.py:27
  108.4 19.6 %reduce-scatter.2.cloned.1.call-done = f32[64,2048]{1,0:T(8,128)} async-done(((f32[64,8192]{1,0:T(8,128)}), f32[64,2048]{1,0:T(8,128)}) %reduce-scatter.2.cloned.1.call-update) | async-done | bytes 524304 | tf_op jit(solution)/shard_map/reduce_scatter | solution.py:57
  128.0 1.1 convert_element_type.54
  129.1 0.0 copy-start.2
  129.1 1.7 gather_fusion.1
  130.8 2.0 reshape_transpose_transpose_reshape_reshape_reshape_reshape.7
  132.8 0.0 all-to-all-done
  132.9 7.7 %all-to-all-start.2 = ((bf16[32,1,1,4,2048]{4,3,2,1,0:T(4,128)(2,1)}), bf16[32,1,1,4,2048]{4,3,2,1,0:T(4,128)(2,1)}, u32[]{:S(2)}, u32[]{:S(2)}) async-start(bf16[32,1,1,4,2048]{4,3,2,1,0:T(4,128)(2,1)} %bitcast.89), calls=%async_computation.3 | async-start | bytes 1048576 | tf_op jit(solution)/shard_map/all_to_all | solution.py:27
  140.5 0.0 all-gather.6.cloned.1.call-start
  140.6 0.0 copy-done.5
  140.6 0.1 copy.45
  140.7 0.1 copy.33
  140.8 0.1 select_n.64
  141.0 10.7 %all-to-all-done.2 = bf16[32,1,1,4,2048]{4,3,2,1,0:T(4,128)(2,1)} async-done(((bf16[32,1,1,4,2048]{4,3,2,1,0:T(4,128)(2,1)}), bf16[32,1,1,4,2048]{4,3,2,1,0:T(4,128)(2,1)}, u32[]{:S(2)}, u32[]{:S(2)}) %all-to-all-start.2) | async-done | bytes 524320 | tf_op jit(solution)/shard_map/all_to_all | solution.py:27
  151.7 2.0 reshape.301
  153.6 0.0 copy-done.2
  153.6 2.4 scatter_fusion
  156.1 0.0 copy-start.1
  156.1 0.3 fusion.7
  156.4 6.9 %psum.7 = f32[256]{0:T(256)S(1)} all-reduce(f32[256]{0:T(256)S(1)} %fusion.7), channel_id=1, replica_groups=mesh['role'=2,'seq'=16,'tp'=4] {'tp'}, use_global_device_ids=true, to_apply=%region_6.7 | all-reduce | flops 256 | bytes 2048 | tf_op jit(solution)/shard_map/psum | solution.py:126
  163.3 1.3 fusion.9
  164.6 0.0 all-gather.6.cloned.1.call-update
  164.6 0.0 all-gather.8.cloned.1.call-start
  164.7 45.9 %all-gather.6.cloned.1.call-done = bf16[256,8192]{1,0:T(8,128)(2,1)} async-done(((bf16[256,2048]{1,0:T(8,128)(2,1)}), bf16[256,8192]{1,0:T(8,128)(2,1)}) %all-gather.6.cloned.1.call-update) | async-done | bytes 4194320 | tf_op jit(solution)/shard_map/all_gather | solution.py:130
  210.6 0.0 copy-done
  210.6 0.0 copy-start.4
  210.6 3.8 %convolution_bitcast_fusion.1 = f32[256,1,128]{0,2,1:T(8,128)S(1)} fusion(bf16[256,8192]{1,0:T(8,128)(2,1)} %all-gather.6.cloned.1.call-done, bf16[8192,128]{1,0:T(8,128)(2,1)S(1)} %copy-done), kind=kOutput, calls=%fused_computation.22 | convolution fusion | flops 536870912 | bytes 6422528 | tf_op jit(solution)/shard_map/dot_general | solution.py:132
  214.4 0.0 copy-done.1
  214.5 0.3 fusion.22
  214.8 0.0 copy-done.3
  214.8 0.0 copy-done.4
  214.8 1.5 fusion.11
  216.3 0.7 pad_maximum_fusion
  217.0 0.0 all-gather.8.cloned.1.call-update
  217.0 0.5 multiply_cosine_fusion
  217.6 2.7 iota_compare_fusion
  220.3 9.5 %convolution_bitcast_fusion = f32[32,8,8,128]{3,1,2,0:T(8,128)S(1)} fusion(bf16[256,8192]{1,0:T(8,128)(2,1)} %all-gather.6.cloned.1.call-done, bf16[8192,1024]{1,0:T(8,128)(2,1)} %param.13), kind=kOutput, calls=%fused_computation.21 | convolution fusion | flops 4294967296 | bytes 22020096 | tf_op jit(solution)/shard_map/dot_general | solution.py:132
  229.8 0.2 copy.50
  230.0 0.3 fusion.34
  230.3 0.4 subtract_convert_fusion
  230.7 36.6 %all-gather.8.cloned.1.call-done = bf16[8192,2,128]{0,2,1:T(8,128)(2,1)} async-done(((bf16[256,2,128]{0,2,1:T(8,128)(2,1)}), bf16[8192,2,128]{0,2,1:T(8,128)(2,1)}) %all-gather.8.cloned.1.call-update) | async-done | bytes 4194320 | tf_op jit(solution)/shard_map/all_gather | solution.py:35
  267.3 25.4 %fusion = (f32[8,256]{1,0:T(8,128)S(1)}, f32[8192,256,8]{1,0,2:T(8,128)}) fusion(pred[256,8192]{0,1:T(8,128)(4,1)} %iota_compare_fusion, bf16[256,8,64]{2,0,1:T(8,128)(2,1)S(1)} %get-tuple-element.9, bf16[256,8,64]{2,0,1:T(8,128)(2,1)S(1)} %get-tuple-element.8, bf16[8192,2,128]{0,2,1:T(8,128)(2,1)} %all-gather.8.cloned.1.call-done), kind=kOutput, calls=%fused_computation.6 | convolution fusion | flops 4346345472 | bytes 71835648 | tf_op jit(solution)/shard_map/qhgd,khd->hgqk/dot_general | solution.py:150
  292.8 22.3 %fusion.1 = f32[8,256]{1,0:T(8,128)S(1)} fusion(f32[8192,256,8]{1,0,2:T(8,128)} %get-tuple-element.17, f32[8,256]{1,0:T(8,128)S(1)} %broadcast_maximum_fusion, pred[256,8192]{0,1:T(8,128)(4,1)} %iota_compare_fusion), kind=kLoop, calls=%fused_computation.7 | loop fusion | flops 83884032 | bytes 69222400 | tf_op jit(solution)/shard_map/reduce_sum | solution.py:158
  315.0 25.3 %divide_convert_fusion = bf16[8,256,128]{1,2,0:T(8,128)(2,1)S(1)} fusion(f32[8192,256,8]{1,0,2:T(8,128)} %get-tuple-element.17, f32[8,256]{1,0:T(8,128)S(1)} %broadcast_maximum_fusion, pred[256,8192]{0,1:T(8,128)(4,1)} %iota_compare_fusion, bf16[8192,2,128]{0,2,1:T(8,128)(2,1)} %all-gather.8.cloned.1.call-done, f32[8,256]{1,0:T(8,128)S(1)} %fusion.1), kind=kOutput, calls=%fused_computation.25 | convolution fusion | flops 4379377664 | bytes 71843840 | tf_op jit(solution)/shard_map/hgqk,khd->hgqd/dot_general | solution.py:159
  340.4 1.0 copy.41
  (16 shorter events, 0.1 us)
Async XLA Ops:
  7.2 203.4 %copy-start = (bf16[8192,128]{1,0:T(8,128)(2,1)S(1)}, bf16[8192,128]{1,0:T(8,128)(2,1)}, u32[]{:S(2)}) copy-start(bf16[8192,128]{1,0:T(8,128)(2,1)} %param.14) | copy-start | bytes 6291460
  7.2 54.3 %all-gather.4.cloned.1.call-start = ((), (), s32[]{:S(2)}) async-start(), calls=%async_computation.4 | async-start | bytes 5406720 | tf_op jit(solution)/shard_map/all_gather | solution.py:64
  7.9 120.1 %reduce-scatter.2.cloned.1.call-start = ((), (), s32[]{:S(2)}) async-start(), calls=%async_computation.5 | async-start | bytes 2621440 | tf_op jit(solution)/shard_map/reduce_scatter | solution.py:57
  98.5 1.5 copy-start.6
  102.6 38.0 %copy-start.5 = (bf16[2048]{0:T(1024)(128)(2,1)S(1)}, bf16[2048]{0:T(1024)(128)(2,1)}, u32[]{:S(2)}) copy-start(bf16[2048]{0:T(1024)(128)(2,1)} %param.12) | copy-start | bytes 12292
  103.3 29.5 %all-to-all-start = ((s32[32,1,1,4]{3,2,1,0:T(1,128)}), s32[32,1,1,4]{3,2,1,0:T(1,128)S(1)}, u32[]{:S(2)}, u32[]{:S(2)}) async-start(s32[32,1,1,4]{3,2,1,0:T(1,128)} %bitcast), calls=%async_computation | async-start | bytes 32768 | tf_op jit(solution)/shard_map/all_to_all | solution.py:27
  129.1 24.6 %copy-start.2 = (bf16[256,2048]{1,0:T(8,128)(2,1)S(1)}, bf16[256,2048]{1,0:T(8,128)(2,1)}, u32[]{:S(2)}) copy-start(bf16[256,2048]{1,0:T(8,128)(2,1)} %param.11) | copy-start | bytes 3145732
  132.9 18.8 %all-to-all-start.2 = ((bf16[32,1,1,4,2048]{4,3,2,1,0:T(4,128)(2,1)}), bf16[32,1,1,4,2048]{4,3,2,1,0:T(4,128)(2,1)}, u32[]{:S(2)}, u32[]{:S(2)}) async-start(bf16[32,1,1,4,2048]{4,3,2,1,0:T(4,128)(2,1)} %bitcast.89), calls=%async_computation.3 | async-start | bytes 1048576 | tf_op jit(solution)/shard_map/all_to_all | solution.py:27
  140.5 70.1 %all-gather.6.cloned.1.call-start = ((), (), s32[]{:S(2)}) async-start(), calls=%async_computation.6 | async-start | bytes 5242880 | tf_op jit(solution)/shard_map/all_gather | solution.py:130
  156.1 58.4 %copy-start.1 = (bf16[256,2048]{1,0:T(8,128)(2,1)}, bf16[256,2048]{1,0:T(8,128)(2,1)S(1)}, u32[]{:S(2)}) copy-start(bf16[256,2048]{1,0:T(8,128)(2,1)S(1)} %scatter_fusion) | copy-start | bytes 3145732
  164.6 102.8 %all-gather.8.cloned.1.call-start = ((), (), s32[]{:S(2)}) async-start(), calls=%async_computation.7 | async-start | bytes 4325376 | tf_op jit(solution)/shard_map/all_gather | solution.py:35
  210.6 4.2 %copy-start.3 = (bf16[256,8192]{1,0:T(8,128)(2,1)S(1)}, bf16[256,8192]{1,0:T(8,128)(2,1)}, u32[]{:S(2)}) copy-start(bf16[256,8192]{1,0:T(8,128)(2,1)} %all-gather.6.cloned.1.call-done) | copy-start | bytes 12582916
  210.6 4.2 %copy-start.4 = (bf16[8192,128]{1,0:T(8,128)(2,1)S(1)}, bf16[8192,128]{1,0:T(8,128)(2,1)}, u32[]{:S(2)}) copy-start(bf16[8192,128]{1,0:T(8,128)(2,1)} %param.15) | copy-start | bytes 6291460
Sparse Core Ops, SparseCore 0:
  10.3 51.1 all-gather.3
  100.2 27.7 reduce-scatter.1
  164.7 45.8 all-gather.5
  217.1 50.1 all-gather.7
where the time goes:
time: 348 us
  waiting for transfers between devices  167 us (48%)
  matrix products  69.8 us (20%)
  blocking collectives  39.7 us (11%)
  other arithmetic  30.1 us (9%)
  local copies, waits for them, and re-layouts  14.2 us (4%)
  between operations  14.1 us (4%)
  starting transfers between devices  12.9 us (4%)
    all_gather x1, waiting for transfers between devices, project_strips(): lax.all_gather(merger_hidden, ('role', 'seq'), axis=0, tiled=True)  53.5 us
    all_gather x1, waiting for transfers between devices, body(): shard_piece = lax.all_gather(normed, 'tp', axis=1, tiled=True)  45.9 us
    all_gather x1, waiting for transfers between devices, sent_together(): filled = lax.all_gather(both, axis, axis=dim, tiled=True)  36.6 us
    all_to_all x1, blocking collectives, body(): lax.all_to_all(strips, ('role', 'seq'), split_axis=0, concat_axis=1, tile...  32.9 us
    dot_general x1, matrix products, body(): jnp.einsum('qhgd,khd->hgqk', queries, key_piece, preferred_element_type=j...  25.4 us
    dot_general x1, matrix products, body(): jnp.einsum('hgqk,khd->hgqd', probability.astype(jnp.bfloat16), value_piec...  25.3 us
    reduce_sum x1, other arithmetic, body(): running_sum = jnp.sum(probability, axis=3)  22.3 us
    reduce_scatter x1, waiting for transfers between devices, sum_hidden(): lax.psum_scatter(partial_value, 'tp', scatter_dimension=1, tiled=True)  19.6 us
  transfers between devices with their start and end apart: 6, of which 5 were waited for; matrix products, arithmetic and copies ran while one was open for 6% of the time, Pallas kernels for 0%

commit v1 on v0

--- a/solution.py
+++ b/solution.py
@@ -61,7 +61,12 @@
 
 def project_strips(merger_hidden, merger_out):
     return jnp.dot(
-        lax.all_gather(merger_hidden, ("role", "seq"), axis=0, tiled=True),
+        jnp.concatenate(
+            lax.all_to_all(
+                jnp.stack([merger_hidden] * lax.axis_size(("role", "seq"))), ("role", "seq"), 0, 0
+            ),
+            axis=0,
+        ),
         merger_out,
         preferred_element_type=jnp.float32,
     )

time: 348 us -> 363 us (1.043)
  blocking collectives: 39.7 us -> 110 us
  waiting for transfers between devices: 167 us -> 113 us
    all_to_all x0 -> x1, blocking collectives: none -> 70.8 us  [project_strips(): lax.all_to_all(jnp.stack([merger_hidden] * lax.axis_size(('role', 'seq'))...]
    all_gather x1 -> x0, waiting for transfers between devices: 53.5 us -> none  [project_strips(): lax.all_gather(merger_hidden, ('role', 'seq'), axis=0, tiled=True)]
  transfers between devices with their start and end apart: 6 -> 5, of which waited for: 5 -> 4; matrix products, arithmetic and copies ran while one was open for 6% -> 6% of each run, Pallas kernels for 0% -> 0%
where the time goes in v1:
time: 363 us
  waiting for transfers between devices  113 us (31%)
  blocking collectives  110 us (30%)
  matrix products  67.2 us (19%)
  other arithmetic  30.1 us (8%)
  local copies, waits for them, and re-layouts  15.9 us (4%)
  between operations  14.1 us (4%)
  starting transfers between devices  13 us (4%)
    all_to_all x1, blocking collectives, project_strips(): lax.all_to_all(jnp.stack([merger_hidden] * lax.axis_size(('role', 'seq'))...  70.8 us
    all_gather x1, waiting for transfers between devices, body(): shard_piece = lax.all_gather(normed, 'tp', axis=1, tiled=True)  45.8 us
    all_gather x1, waiting for transfers between devices, sent_together(): filled = lax.all_gather(both, axis, axis=dim, tiled=True)  36.6 us
    all_to_all x1, blocking collectives, body(): lax.all_to_all(strips, ('role', 'seq'), split_axis=0, concat_axis=1, tile...  32 us
    dot_general x1, matrix products, body(): jnp.einsum('qhgd,khd->hgqk', queries, key_piece, preferred_element_type=j...  25.4 us
    dot_general x1, matrix products, body(): jnp.einsum('hgqk,khd->hgqd', probability.astype(jnp.bfloat16), value_piec...  25.4 us
    reduce_sum x1, other arithmetic, body(): running_sum = jnp.sum(probability, axis=3)  22.3 us
    reduce_scatter x1, waiting for transfers between devices, sum_hidden(): lax.psum_scatter(partial_value, 'tp', scatter_dimension=1, tiled=True)  19.9 us
  transfers between devices with their start and end apart: 5, of which 4 were waited for; matrix products, arithmetic and copies ran while one was open for 6% of the time, Pallas kernels for 0%

profile of v1, /device:TPU:1, one launch (start us, length us, event | category | flops | bytes accessed | tf_op | source)
XLA Modules:
  0.0 362.9 jit_solution(14864263121105532357)
XLA Ops:
  7.2 0.0 copy-start
  7.2 0.0 reduce-scatter.2.cloned.1.call-start
  7.2 1.6 stack.2
  8.9 0.0 copy-start.6
  8.9 70.8 %all_to_all.31 = bf16[32,64,1280]{2,1,0:T(8,128)(2,1)S(1)} all-to-all(bf16[32,64,1280]{2,1,0:T(8,128)(2,1)S(1)} %stack.2), channel_id=1, replica_groups=mesh['role'=2,'seq'=16,'tp'=4] {'role','seq'}, dimensions={0} | all-to-all | bytes 10485760 | tf_op jit(solution)/shard_map/all_to_all | solution.py:65
  79.7 0.0 copy-done.6
  79.7 1.6 fusion.14
  81.3 32.0 %all_to_all.32 = f32[32,64,256]{2,1,0:T(8,128)S(1)} all-to-all(f32[32,64,256]{2,1,0:T(8,128)S(1)} %fusion.14), channel_id=1, replica_groups=mesh['role'=2,'seq'=16,'tp'=4] {'role','seq'}, dimensions={0} | all-to-all | bytes 4194304 | tf_op jit(solution)/shard_map/all_to_all | solution.py:93
  113.3 0.0 copy-start.7
  113.3 1.5 copy.48
  114.9 0.0 reduce-scatter.2.cloned.1.call-update
  114.9 0.0 copy-done.7
  114.9 0.1 fusion.27
  115.0 0.1 reduce_window_sum.11
  115.1 0.2 select_reduce_fusion
  115.3 0.8 scatter_custom_fusion
  116.1 0.1 pad_add_fusion
  116.2 1.2 gather_fusion
  117.4 0.0 copy-start.5
  117.4 0.7 reshape_transpose_transpose_reshape_reshape_reshape_reshape.6
  118.1 5.0 %all-to-all-start = ((s32[32,1,1,4]{3,2,1,0:T(1,128)}), s32[32,1,1,4]{3,2,1,0:T(1,128)S(1)}, u32[]{:S(2)}, u32[]{:S(2)}) async-start(s32[32,1,1,4]{3,2,1,0:T(1,128)} %bitcast), calls=%async_computation | async-start | bytes 32768 | tf_op jit(solution)/shard_map/all_to_all | solution.py:27
  123.1 19.9 %reduce-scatter.2.cloned.1.call-done = f32[64,2048]{1,0:T(8,128)} async-done(((f32[64,8192]{1,0:T(8,128)}), f32[64,2048]{1,0:T(8,128)}) %reduce-scatter.2.cloned.1.call-update) | async-done | bytes 524304 | tf_op jit(solution)/shard_map/reduce_scatter | solution.py:57
  143.0 1.1 convert_element_type.54
  144.0 0.0 copy-start.2
  144.1 1.7 gather_fusion.1
  145.8 2.0 reshape_transpose_transpose_reshape_reshape_reshape_reshape.7
  147.8 0.0 all-to-all-done
  147.8 7.7 %all-to-all-start.3 = ((bf16[32,1,1,4,2048]{4,3,2,1,0:T(4,128)(2,1)}), bf16[32,1,1,4,2048]{4,3,2,1,0:T(4,128)(2,1)}, u32[]{:S(2)}, u32[]{:S(2)}) async-start(bf16[32,1,1,4,2048]{4,3,2,1,0:T(4,128)(2,1)} %bitcast.89), calls=%async_computation.4 | async-start | bytes 1048576 | tf_op jit(solution)/shard_map/all_to_all | solution.py:27
  155.5 0.0 all-gather.3.cloned.1.call-start
  155.6 0.0 copy-done.5
  155.6 0.1 copy.44
  155.7 0.1 copy.32
  155.8 0.1 select_n.64
  155.9 10.7 %all-to-all-done.3 = bf16[32,1,1,4,2048]{4,3,2,1,0:T(4,128)(2,1)} async-done(((bf16[32,1,1,4,2048]{4,3,2,1,0:T(4,128)(2,1)}), bf16[32,1,1,4,2048]{4,3,2,1,0:T(4,128)(2,1)}, u32[]{:S(2)}, u32[]{:S(2)}) %all-to-all-start.3) | async-done | bytes 524320 | tf_op jit(solution)/shard_map/all_to_all | solution.py:27
  166.7 2.0 reshape.306
  168.6 0.0 copy-done.2
  168.6 2.4 scatter_fusion
  171.1 0.0 copy-start.1
  171.1 0.3 fusion.7
  171.4 6.9 %psum.7 = f32[256]{0:T(256)S(1)} all-reduce(f32[256]{0:T(256)S(1)} %fusion.7), channel_id=1, replica_groups=mesh['role'=2,'seq'=16,'tp'=4] {'tp'}, use_global_device_ids=true, to_apply=%region_6.7 | all-reduce | flops 256 | bytes 2048 | tf_op jit(solution)/shard_map/psum | solution.py:131
  178.3 1.3 fusion.9
  179.5 0.0 all-gather.3.cloned.1.call-update
  179.6 0.2 all-gather.5.cloned.1.call-start
  179.8 45.8 %all-gather.3.cloned.1.call-done = bf16[256,8192]{1,0:T(8,128)(2,1)} async-done(((bf16[256,2048]{1,0:T(8,128)(2,1)}), bf16[256,8192]{1,0:T(8,128)(2,1)}) %all-gather.3.cloned.1.call-update) | async-done | bytes 4194320 | tf_op jit(solution)/shard_map/all_gather | solution.py:135
  225.6 0.0 copy-done
  225.6 3.8 %convolution_bitcast_fusion.1 = f32[256,1,128]{0,2,1:T(8,128)S(1)} fusion(bf16[256,8192]{1,0:T(8,128)(2,1)} %all-gather.3.cloned.1.call-done, bf16[8192,128]{1,0:T(8,128)(2,1)S(1)} %copy-done), kind=kOutput, calls=%fused_computation.22 | convolution fusion | flops 536870912 | bytes 6422528 | tf_op jit(solution)/shard_map/dot_general | solution.py:137
  229.4 0.0 copy-done.1
  229.4 0.3 fusion.24
  229.8 0.0 copy-done.3
  229.8 0.0 copy-done.4
  229.8 1.5 fusion.11
  231.3 0.7 pad_maximum_fusion
  232.0 0.0 all-gather.5.cloned.1.call-update
  232.0 0.5 multiply_cosine_fusion
  232.6 2.7 iota_compare_fusion
  235.3 9.5 %convolution_bitcast_fusion = f32[32,8,8,128]{3,1,2,0:T(8,128)S(1)} fusion(bf16[256,8192]{1,0:T(8,128)(2,1)} %all-gather.3.cloned.1.call-done, bf16[8192,1024]{1,0:T(8,128)(2,1)} %param.13), kind=kOutput, calls=%fused_computation.21 | convolution fusion | flops 4294967296 | bytes 22020096 | tf_op jit(solution)/shard_map/dot_general | solution.py:137
  244.8 0.2 copy.49
  245.0 0.3 fusion.36
  245.3 0.4 subtract_convert_fusion
  245.7 36.6 %all-gather.5.cloned.1.call-done = bf16[8192,2,128]{0,2,1:T(8,128)(2,1)} async-done(((bf16[256,2,128]{0,2,1:T(8,128)(2,1)}), bf16[8192,2,128]{0,2,1:T(8,128)(2,1)}) %all-gather.5.cloned.1.call-update) | async-done | bytes 4194320 | tf_op jit(solution)/shard_map/all_gather | solution.py:35
  282.3 25.4 %fusion = (f32[8,256]{1,0:T(8,128)S(1)}, f32[8192,256,8]{1,0,2:T(8,128)}) fusion(pred[256,8192]{0,1:T(8,128)(4,1)} %iota_compare_fusion, bf16[256,8,64]{2,0,1:T(8,128)(2,1)S(1)} %get-tuple-element.9, bf16[256,8,64]{2,0,1:T(8,128)(2,1)S(1)} %get-tuple-element.8, bf16[8192,2,128]{0,2,1:T(8,128)(2,1)} %all-gather.5.cloned.1.call-done), kind=kOutput, calls=%fused_computation.6 | convolution fusion | flops 4346345472 | bytes 71835648 | tf_op jit(solution)/shard_map/qhgd,khd->hgqk/dot_general | solution.py:155
  307.7 22.3 %fusion.1 = f32[8,256]{1,0:T(8,128)S(1)} fusion(f32[8192,256,8]{1,0,2:T(8,128)} %get-tuple-element.17, f32[8,256]{1,0:T(8,128)S(1)} %broadcast_maximum_fusion, pred[256,8192]{0,1:T(8,128)(4,1)} %iota_compare_fusion), kind=kLoop, calls=%fused_computation.7 | loop fusion | flops 83884032 | bytes 69222400 | tf_op jit(solution)/shard_map/reduce_sum | solution.py:163
  330.0 25.4 %divide_convert_fusion = bf16[8,256,128]{1,2,0:T(8,128)(2,1)S(1)} fusion(f32[8192,256,8]{1,0,2:T(8,128)} %get-tuple-element.17, f32[8,256]{1,0:T(8,128)S(1)} %broadcast_maximum_fusion, pred[256,8192]{0,1:T(8,128)(4,1)} %iota_compare_fusion, bf16[8192,2,128]{0,2,1:T(8,128)(2,1)} %all-gather.5.cloned.1.call-done, f32[8,256]{1,0:T(8,128)S(1)} %fusion.1), kind=kOutput, calls=%fused_computation.25 | convolution fusion | flops 4379377664 | bytes 71843840 | tf_op jit(solution)/shard_map/hgqk,khd->hgqd/dot_general | solution.py:164
  355.4 1.0 copy.40
  (17 shorter events, 0.1 us)
Async XLA Ops:
  7.2 218.4 %copy-start = (bf16[8192,128]{1,0:T(8,128)(2,1)S(1)}, bf16[8192,128]{1,0:T(8,128)(2,1)}, u32[]{:S(2)}) copy-start(bf16[8192,128]{1,0:T(8,128)(2,1)} %param.14) | copy-start | bytes 6291460
  7.2 135.8 %reduce-scatter.2.cloned.1.call-start = ((), (), s32[]{:S(2)}) async-start(), calls=%async_computation.5 | async-start | bytes 2621440 | tf_op jit(solution)/shard_map/reduce_scatter | solution.py:57
  8.9 70.9 %copy-start.6 = (bf16[1280,256]{1,0:T(8,128)(2,1)S(1)}, bf16[1280,256]{1,0:T(8,128)(2,1)}, u32[]{:S(2)}) copy-start(bf16[1280,256]{1,0:T(8,128)(2,1)} %param.9) | copy-start | bytes 1966084
  113.3 1.5 copy-start.7
  117.4 38.2 %copy-start.5 = (bf16[2048]{0:T(1024)(128)(2,1)S(1)}, bf16[2048]{0:T(1024)(128)(2,1)}, u32[]{:S(2)}) copy-start(bf16[2048]{0:T(1024)(128)(2,1)} %param.12) | copy-start | bytes 12292
  118.1 29.7 %all-to-all-start = ((s32[32,1,1,4]{3,2,1,0:T(1,128)}), s32[32,1,1,4]{3,2,1,0:T(1,128)S(1)}, u32[]{:S(2)}, u32[]{:S(2)}) async-start(s32[32,1,1,4]{3,2,1,0:T(1,128)} %bitcast), calls=%async_computation | async-start | bytes 32768 | tf_op jit(solution)/shard_map/all_to_all | solution.py:27
  144.0 24.6 %copy-start.2 = (bf16[256,2048]{1,0:T(8,128)(2,1)S(1)}, bf16[256,2048]{1,0:T(8,128)(2,1)}, u32[]{:S(2)}) copy-start(bf16[256,2048]{1,0:T(8,128)(2,1)} %param.11) | copy-start | bytes 3145732
  147.8 18.8 %all-to-all-start.3 = ((bf16[32,1,1,4,2048]{4,3,2,1,0:T(4,128)(2,1)}), bf16[32,1,1,4,2048]{4,3,2,1,0:T(4,128)(2,1)}, u32[]{:S(2)}, u32[]{:S(2)}) async-start(bf16[32,1,1,4,2048]{4,3,2,1,0:T(4,128)(2,1)} %bitcast.89), calls=%async_computation.4 | async-start | bytes 1048576 | tf_op jit(solution)/shard_map/all_to_all | solution.py:27
  155.5 70.1 %all-gather.3.cloned.1.call-start = ((), (), s32[]{:S(2)}) async-start(), calls=%async_computation.6 | async-start | bytes 5242880 | tf_op jit(solution)/shard_map/all_gather | solution.py:135
  171.1 58.4 %copy-start.1 = (bf16[256,2048]{1,0:T(8,128)(2,1)}, bf16[256,2048]{1,0:T(8,128)(2,1)S(1)}, u32[]{:S(2)}) copy-start(bf16[256,2048]{1,0:T(8,128)(2,1)S(1)} %scatter_fusion) | copy-start | bytes 3145732
  179.6 102.8 %all-gather.5.cloned.1.call-start = ((), (), s32[]{:S(2)}) async-start(), calls=%async_computation.7 | async-start | bytes 4325376 | tf_op jit(solution)/shard_map/all_gather | solution.py:35
  225.6 4.2 %copy-start.3 = (bf16[256,8192]{1,0:T(8,128)(2,1)S(1)}, bf16[256,8192]{1,0:T(8,128)(2,1)}, u32[]{:S(2)}) copy-start(bf16[256,8192]{1,0:T(8,128)(2,1)} %all-gather.3.cloned.1.call-done) | copy-start | bytes 12582916
  225.6 4.2 %copy-start.4 = (bf16[8192,128]{1,0:T(8,128)(2,1)S(1)}, bf16[8192,128]{1,0:T(8,128)(2,1)}, u32[]{:S(2)}) copy-start(bf16[8192,128]{1,0:T(8,128)(2,1)} %param.15) | copy-start | bytes 6291460
Sparse Core Ops, SparseCore 0:
  115.0 27.9 reduce-scatter.1
  179.7 45.8 all-gather.2
  232.1 50.1 all-gather.4
